TPU v7x, 32 devices: a whole 2x2x4 slice. The times are simulated.
32 devices in a mesh: segment: 2 (over core), expert: 8 (over z, y), dp: 2 (over x).
Axes of the slice: x: 2, y: 2, z: 4, core: 2. Of those that a mesh axis runs over, the one named last changes fastest.
Arguments:
- moe_input: bfloat16 [2, 1024, 2688], P('segment', 'expert', 'dp'), may hold values from -64 to 64
- norm_gain: float32 [2688], replicated, may hold values from 0.1 to 1.9
- routes: int32 [2, 1024, 6], P('segment', 'expert'), may hold values from 0 to 15, all different within a row; in each aligned block of 128 rows (0 to 127, 128 to 255, ..., all dimensions but the last counted through in order) at most 54 rows name the same one
- route_scores: float32 [2, 1024, 6], P('segment', 'expert'), may hold values from -8 to 8
- w_up: bfloat16 [16, 2688, 1856], P('expert', None, 'dp'), may hold values from -0.125 to 0.125
- w_down: bfloat16 [16, 1856, 2688], P('expert', None, 'dp'), may hold values from -0.125 to 0.125
- queries: bfloat16 [2, 1024, 2048], P('segment', 'expert', 'dp'), may hold values from -100 to 100
- keys: bfloat16 [2, 1024, 256], P('segment', 'expert'), may hold values from -6 to 6
- values: bfloat16 [2, 1024, 256], P('segment', 'expert'), may hold values from -6 to 6
- out_grad: bfloat16 [2, 1024, 2688], P('segment', 'expert'), may hold values from -6 to 6
- w_query: bfloat16 [2688, 2048], P(None, 'dp'), may hold values from -0.125 to 0.125
- w_key: bfloat16 [2688, 256], replicated, may hold values from -0.125 to 0.125
- w_value: bfloat16 [2688, 256], replicated, may hold values from -0.125 to 0.125
- w_out: bfloat16 [2048, 2688], P('dp'), may hold values from -0.125 to 0.125
Outputs:
- moe_next: bfloat16 [2, 1024, 2688], P('segment', 'expert', 'dp')
- grad_prev: bfloat16 [2, 1024, 2688], P('segment', 'expert', 'dp')
Inputs may be any that keep to these rules, and one draw needn't show every extreme that they name: `routes`: each row names 6 different experts. Among the 128 rows of one sequence no expert is named more than 54 times, a bound that some block reaches; every expert is named by some row.
All inputs are finite; a program needn't handle non-finite values.
Results may differ from a plain program's by a relative error of at most 0.028.
Values may be sent and summed in bfloat16 or wider, within the bound.
No kernel may reach another device: no remote copies, remote signals or barrier semaphores. Data moves between devices by JAX's collectives and lax.ppermute only.
A program may use at most 128 MiB of HBM per device.

v0:
```python
import jax
import jax.numpy as jnp
from jax import lax
from jax.sharding import PartitionSpec as P

D = 2688
HEADS = 16
KV_HEADS = 2
HEAD_DIM = 128
TOPK = 6
NORM_EPSILON = 1e-05


def partner(block, axis, distance):
    count = lax.axis_size(axis)
    route = []
    for low in range(count):
        high = low | 1 << distance
        if high != low and high < count:
            route += [(low, high), (high, low)]
    return lax.ppermute(block, axis, route)


def attention_grad(queries, keys, values, out_grad, w_query, w_key, w_value, w_out, block_index):
    token_count = queries.shape[0]
    query_width = queries.shape[1]
    heads_here = query_width // HEAD_DIM
    group_size = HEADS // KV_HEADS
    score_scale = HEAD_DIM ** (-0.5)
    head_group = block_index * heads_here // group_size
    kv_start = head_group * HEAD_DIM
    key_head = lax.dynamic_slice_in_dim(keys, kv_start, HEAD_DIM, 1)
    value_head = lax.dynamic_slice_in_dim(values, kv_start, HEAD_DIM, 1)
    key_weight = lax.dynamic_slice_in_dim(w_key, kv_start, HEAD_DIM, 1)
    value_weight = lax.dynamic_slice_in_dim(w_value, kv_start, HEAD_DIM, 1)
    d_attn = jnp.einsum("td,qd->tq", out_grad, w_out, preferred_element_type=jnp.float32).astype(
        jnp.bfloat16
    )
    grad_heads = d_attn.reshape(token_count, heads_here, HEAD_DIM)
    query_heads = queries.reshape(token_count, heads_here, HEAD_DIM)
    scores = (
        jnp.einsum("ihd,jd->hij", query_heads, key_head, preferred_element_type=jnp.float32)
        * score_scale
    )
    positions = jnp.arange(token_count, dtype=jnp.int32)
    causal = positions[None, :] <= positions[:, None]
    scores = jnp.where(causal[None], scores, -jnp.inf)
    peak = jnp.max(scores, axis=2, keepdims=True)
    raised = jnp.exp(scores - peak)
    attn_weights = raised / jnp.sum(raised, axis=2, keepdims=True)
    d_weights = jnp.einsum(
        "ihd,jd->hij", grad_heads, value_head, preferred_element_type=jnp.float32
    )
    row_delta = jnp.sum(attn_weights * d_weights, axis=2, keepdims=True)
    d_scores = (attn_weights * (d_weights - row_delta)).astype(jnp.bfloat16)
    d_query = (
        jnp.einsum("hij,jd->ihd", d_scores, key_head, preferred_element_type=jnp.float32)
        * score_scale
    )
    d_query = d_query.astype(jnp.bfloat16).reshape(token_count, query_width)
    d_key = (
        jnp.einsum("hij,ihd->jd", d_scores, query_heads, preferred_element_type=jnp.float32)
        * score_scale
    ).astype(jnp.bfloat16)
    d_value = jnp.einsum(
        "hij,ihd->jd",
        attn_weights.astype(jnp.bfloat16),
        grad_heads,
        preferred_element_type=jnp.float32,
    ).astype(jnp.bfloat16)
    grad_term = jnp.einsum("tq,dq->td", d_query, w_query, preferred_element_type=jnp.float32)
    grad_term = grad_term + jnp.einsum(
        "tk,dk->td", d_key, key_weight, preferred_element_type=jnp.float32
    )
    grad_term = grad_term + jnp.einsum(
        "tk,dk->td", d_value, value_weight, preferred_element_type=jnp.float32
    )
    return grad_term


def block_product(block_rows, w_up, first_feature):
    width = block_rows.shape[3]
    weight_rows = lax.dynamic_slice_in_dim(w_up, first_feature, width, 1)
    product = jnp.einsum(
        "sjcw,jwh->sjch", block_rows, weight_rows, preferred_element_type=jnp.float32
    )
    return lax.optimization_barrier(product.astype(jnp.bfloat16)).astype(jnp.float32)


def on_device(
    moe_input,
    norm_gain,
    routes,
    route_scores,
    w_up,
    w_down,
    queries,
    keys,
    values,
    out_grad,
    w_query,
    w_key,
    w_value,
    w_out,
):
    columns = lax.axis_size("expert")
    token_count = moe_input.shape[1]
    feature_share = moe_input.shape[2]
    local_experts = w_up.shape[0]
    hidden_share = w_up.shape[2]
    expert_count = local_experts * columns
    capacity = (9 * token_count * TOPK + 8 * expert_count - 1) // (8 * expert_count)
    slot_count = expert_count * capacity
    feature_index = lax.axis_index("dp")
    token_rows = moe_input[0]
    chosen_experts = routes[0]
    logits = route_scores[0]
    flat_choices = chosen_experts.reshape(-1)
    expert_hits = (
        flat_choices[:, None] == jnp.arange(expert_count, dtype=jnp.int32)[None, :]
    ).astype(jnp.int32)
    earlier = jnp.cumsum(expert_hits, axis=0) - expert_hits
    places = jnp.sum(earlier * expert_hits, axis=1).reshape(token_count, TOPK)
    targets = chosen_experts * capacity + places
    slot_ids = jnp.arange(slot_count, dtype=jnp.int32)
    signal = jax.nn.sigmoid(logits)
    gate_values = (
        (signal / jnp.sum(signal, axis=1, keepdims=True)).astype(jnp.bfloat16).astype(jnp.float32)
    )
    spread_sum = jnp.zeros((token_count, slot_count), jnp.float32)
    mixing_sum = jnp.zeros((token_count, slot_count), jnp.float32)
    for choice_index in range(TOPK):
        hit = slot_ids[None, :] == targets[:, choice_index : choice_index + 1]
        spread_sum = spread_sum + hit.astype(jnp.float32)
        mixing_sum = mixing_sum + jnp.where(
            hit, gate_values[:, choice_index : choice_index + 1], 0.0
        )
    spread = spread_sum.astype(jnp.bfloat16)
    mixing = mixing_sum.astype(jnp.bfloat16)
    outgoing = jnp.einsum(
        "ts,tw->sw", spread, token_rows, preferred_element_type=jnp.float32
    ).astype(jnp.bfloat16)
    outgoing = outgoing.reshape(columns, local_experts, capacity, feature_share)
    arrived = lax.all_to_all(outgoing, "expert", split_axis=0, concat_axis=0, tiled=True)
    arrived_wide = arrived.astype(jnp.float32)
    start_up = jnp.zeros((columns, local_experts, capacity, hidden_share), jnp.float32)
    squares = lax.psum(jnp.sum(jnp.square(arrived_wide), axis=3), "dp")
    gain_part = lax.dynamic_slice_in_dim(norm_gain, feature_index * feature_share, feature_share, 0)
    scaled = (arrived_wide * gain_part).astype(jnp.bfloat16)
    running = start_up
    piece = lax.all_gather(scaled, "dp", axis=3, tiled=True)
    start = jnp.int32(0)
    for block_number in range(piece.shape[3] // feature_share):
        first = block_number * feature_share
        running = running + block_product(
            piece[:, :, :, first : first + feature_share], w_up, start + first
        )
    inverse = 1.0 / jnp.sqrt(squares / D + NORM_EPSILON)
    projected = running * inverse[..., None]
    hidden = jnp.square(jnp.maximum(projected, 0.0)).astype(jnp.bfloat16)
    grad_term = attention_grad(
        queries[0], keys[0], values[0], out_grad[0], w_query, w_key, w_value, w_out, feature_index
    )
    grad_here = lax.psum_scatter(
        grad_term.astype(jnp.bfloat16), "dp", scatter_dimension=1, tiled=True
    )
    expert_out = jnp.einsum(
        "sjch,jhd->sjcd",
        lax.all_gather(hidden, "dp", axis=3, tiled=True),
        w_down,
        preferred_element_type=jnp.float32,
    )
    expert_rows = expert_out.astype(jnp.bfloat16)
    returned = lax.all_to_all(expert_rows, "expert", split_axis=0, concat_axis=0, tiled=True)
    moe_out = jnp.dot(
        mixing, returned.reshape(slot_count, feature_share), preferred_element_type=jnp.float32
    ).astype(jnp.bfloat16)
    moe_next, grad_prev = partner((moe_out, grad_here), "segment", 0)
    return (moe_next[None], grad_prev[None])


def solution(mesh):
    return jax.shard_map(
        on_device,
        mesh=mesh,
        in_specs=(
            P("segment", "expert", "dp"),
            P(),
            P("segment", "expert", None),
            P("segment", "expert", None),
            P("expert", None, "dp"),
            P("expert", None, "dp"),
            P("segment", "expert", "dp"),
            P("segment", "expert", None),
            P("segment", "expert", None),
            P("segment", "expert", None),
            P(None, "dp"),
            P(),
            P(),
            P("dp", None),
        ),
        out_specs=(P("segment", "expert", "dp"), P("segment", "expert", "dp")),
        check_vma=False,
    )
```

profile of v0, /device:TPU:0, one launch (start us, length us, event | category | flops | bytes accessed | tf_op | source)
XLA Modules:
  0.0 497.4 jit_solution(2547123518346177844)
XLA Ops:
  7.2 0.9 copy.82
  8.4 1.7 reduce-window.6
  11.5 3.5 convolution_convert_fusion
  15.0 21.9 %reshape.76 = bf16[8,2,54,1344]{2,1,0,3:T(2,128)(2,1)} reshape(bf16[864,1344]{0,1:T(8,128)(2,1)} %convolution_convert_fusion) | data formatting | bytes 4644864 | tf_op jit(solution)/shard_map/reshape | solution.py:143
  36.8 15.1 %copy.87 = bf16[8,2,54,1344]{3,1,2,0:T(2,128)(2,1)} copy(bf16[8,2,54,1344]{2,1,0,3:T(2,128)(2,1)} %reshape.76) | data formatting | bytes 4644864 | tf_op jit(solution)/shard_map/reshape | solution.py:143
  52.0 7.4 %all-to-all-start = ((bf16[8,2,54,1344]{3,1,2,0:T(2,128)(2,1)}), bf16[8,2,54,1344]{3,1,2,0:T(2,128)(2,1)}, u32[]{:S(2)}, u32[]{:S(2)}) async-start(bf16[8,2,54,1344]{3,1,2,0:T(2,128)(2,1)} %copy.87), calls=%async_computation | async-start | bytes 4866048 | tf_op jit(solution)/shard_map/all_to_all | solution.py:144
  59.5 55.4 %all-to-all-done = bf16[8,2,54,1344]{3,1,2,0:T(2,128)(2,1)} async-done(((bf16[8,2,54,1344]{3,1,2,0:T(2,128)(2,1)}), bf16[8,2,54,1344]{3,1,2,0:T(2,128)(2,1)}, u32[]{:S(2)}, u32[]{:S(2)}) %all-to-all-start) | async-done | bytes 2322464 | tf_op jit(solution)/shard_map/all_to_all | solution.py:144
  114.9 3.9 fusion.13
  118.8 8.9 %copy.89 = bf16[8,2,54,1344]{2,0,1,3:T(8,128)(2,1)} copy(bf16[8,2,54,1344]{3,0,2,1:T(8,128)(2,1)} %get-tuple-element.11) | data formatting | bytes 4644864 | tf_op jit(solution)/shard_map/convert_element_type | solution.py:149
  127.9 5.0 psum.7
  132.9 129.3 %all-gather.3.cloned.1.call-done = bf16[8,2,54,2688]{2,0,1,3:T(8,128)(2,1)} async-done(((bf16[8,2,54,1344]{2,0,1,3:T(8,128)(2,1)}), bf16[8,2,54,2688]{2,0,1,3:T(8,128)(2,1)}) %all-gather.3.cloned.1.call-update) | async-done | bytes 4644880 | tf_op jit(solution)/shard_map/all_gather | solution.py:151
  262.2 5.5 %fusion.112 = (bf16[8,2,54,1344]{2,0,1,3:T(8,128)(2,1)S(1)}, bf16[8,2,54,1344]{2,0,1,3:T(8,128)(2,1)S(1)}) fusion(bf16[8,2,54,2688]{2,0,1,3:T(8,128)(2,1)} %all-gather.3.cloned.1.call-done), kind=kLoop, calls=%fused_computation.132 | loop fusion | bytes 9289728 | tf_op jit(solution)/shard_map/slice | solution.py:156
  267.7 11.1 %convert_bitcast_fusion.1 = bf16[8,2,54,928]{3,2,0,1:T(8,128)(2,1)} fusion(bf16[2,2688,928]{1,2,0:T(8,128)(2,1)} %param.18, bf16[8,2,54,1344]{2,0,1,3:T(8,128)(2,1)S(1)} %get-tuple-element.8), kind=kOutput, calls=%fused_computation.25 | convolution fusion | flops 2156018688 | bytes 9152512 | tf_op jit(solution)/shard_map/sjcw,jwh->sjch/dot_general | solution.py:84
  278.9 10.0 %convert_bitcast_fusion = bf16[8,2,54,928]{3,2,0,1:T(8,128)(2,1)S(1)} fusion(bf16[2,2688,928]{1,2,0:T(8,128)(2,1)} %param.18, bf16[8,2,54,1344]{2,0,1,3:T(8,128)(2,1)S(1)} %get-tuple-element.9), kind=kOutput, calls=%fused_computation.24 | convolution fusion | flops 2156018688 | bytes 9152512 | tf_op jit(solution)/shard_map/sjcw,jwh->sjch/dot_general | solution.py:84
  288.9 0.8 multiply_convert_fusion
  289.7 4.9 copy.94
  294.7 95.3 %all-gather.5.cloned.1.call-done = bf16[8,2,54,1856]{2,0,1,3:T(8,128)(2,1)} async-done(((bf16[8,2,54,928]{2,0,1,3:T(8,128)(2,1)}), bf16[8,2,54,1856]{2,0,1,3:T(8,128)(2,1)}) %all-gather.5.cloned.1.call-update) | async-done | bytes 3207184 | tf_op jit(solution)/shard_map/all_gather | solution.py:169
  389.9 20.2 %fusion.20 = bf16[8,2,54,1344]{3,2,0,1:T(8,128)(2,1)} fusion(bf16[2,1856,1344]{1,2,0:T(8,128)(2,1)} %param.19, bf16[8,2,54,1856]{2,0,1,3:T(8,128)(2,1)} %all-gather.5.cloned.1.call-done), kind=kOutput, calls=%fused_computation.22 | convolution fusion | flops 4311595008 | bytes 15507456 | tf_op jit(solution)/shard_map/sjch,jhd->sjcd/dot_general | solution.py:167
  410.1 5.7 %copy.96 = bf16[8,2,54,1344]{3,1,2,0:T(2,128)(2,1)} copy(bf16[8,2,54,1344]{3,2,0,1:T(8,128)(2,1)} %fusion.20) | data formatting | bytes 4644864 | tf_op jit(solution)/shard_map/convert_element_type | solution.py:173
  415.8 5.6 %all-to-all-start.1 = ((bf16[8,2,54,1344]{3,1,2,0:T(2,128)(2,1)}), bf16[8,2,54,1344]{3,1,2,0:T(2,128)(2,1)}, u32[]{:S(2)}, u32[]{:S(2)}) async-start(bf16[8,2,54,1344]{3,1,2,0:T(2,128)(2,1)} %copy.96), calls=%async_computation.1 | async-start | bytes 4866048 | tf_op jit(solution)/shard_map/all_to_all | solution.py:174
  422.2 4.4 fusion.38
  427.0 1.0 fusion.37
  427.9 1.6 fusion.42
  429.6 4.6 convolution_add_fusion
  434.2 2.5 fusion.14
  436.9 16.7 %reduce-scatter.2.cloned.1.call-done = bf16[128,1344]{0,1:T(8,128)(2,1)} async-done(((bf16[128,2688]{0,1:T(8,128)(2,1)}), bf16[128,1344]{0,1:T(8,128)(2,1)}) %reduce-scatter.2.cloned.1.call-update) | async-done | bytes 344080 | tf_op jit(solution)/shard_map/reduce_scatter | solution.py:164
  453.5 23.2 %all-to-all-done.1 = bf16[8,2,54,1344]{3,1,2,0:T(2,128)(2,1)} async-done(((bf16[8,2,54,1344]{3,1,2,0:T(2,128)(2,1)}), bf16[8,2,54,1344]{3,1,2,0:T(2,128)(2,1)}, u32[]{:S(2)}, u32[]{:S(2)}) %all-to-all-start.1) | async-done | bytes 2322464 | tf_op jit(solution)/shard_map/all_to_all | solution.py:174
  476.8 3.5 copy.97
  480.3 4.4 reshape.65
  484.7 3.0 convolution_convert_fusion.1
  487.8 1.6 collective-permute-done
  489.4 0.7 copy.171
  (63 shorter events, 3.9 us)
Async XLA Ops:
  7.2 420.8 %copy-start = (bf16[2688,256]{1,0:T(8,128)(2,1)S(1)}, bf16[2688,256]{1,0:T(8,128)(2,1)}, u32[]{:S(2)}) copy-start(bf16[2688,256]{1,0:T(8,128)(2,1)} %param.25) | copy-start | bytes 4128772
  10.9 0.5 copy-start.7
  10.9 0.5 copy-start.9
  10.9 0.5 copy-start.11
  11.0 0.6 copy-start.13
  51.9 7.5 %copy-start.5 = (f32[2688]{0:T(1024)S(1)}, f32[2688]{0:T(1024)}, u32[]{:S(2)}) copy-start(f32[2688]{0:T(1024)} %param.15) | copy-start | bytes 32260
  52.0 63.0 %all-to-all-start = ((bf16[8,2,54,1344]{3,1,2,0:T(2,128)(2,1)}), bf16[8,2,54,1344]{3,1,2,0:T(2,128)(2,1)}, u32[]{:S(2)}, u32[]{:S(2)}) async-start(bf16[8,2,54,1344]{3,1,2,0:T(2,128)(2,1)} %copy.87), calls=%async_computation | async-start | bytes 4866048 | tf_op jit(solution)/shard_map/all_to_all | solution.py:144
  59.4 202.8 %all-gather.3.cloned.1.call-start = ((), (), s32[]{:S(2)}) async-start(), calls=%async_computation.3 | async-start | bytes 16515072 | tf_op jit(solution)/shard_map/all_gather | solution.py:151
  127.8 262.2 %all-gather.5.cloned.1.call-start = ((), (), s32[]{:S(2)}) async-start(), calls=%async_computation.4 | async-start | bytes 11403264 | tf_op jit(solution)/shard_map/all_gather | solution.py:169
  278.9 10.1 %copy-start.1 = (bf16[8,2,54,928]{3,2,0,1:T(8,128)(2,1)S(1)}, bf16[8,2,54,928]{3,2,0,1:T(8,128)(2,1)}, u32[]{:S(2)}) copy-start(bf16[8,2,54,928]{3,2,0,1:T(8,128)(2,1)} %convert_bitcast_fusion.1) | copy-start | bytes 4810756
  415.8 6.0 %copy-start.3 = (bf16[1,128,1024]{2,1,0:T(8,128)(2,1)S(1)}, bf16[1,128,1024]{2,1,0:T(8,128)(2,1)}, u32[]{:S(2)}) copy-start(bf16[1,128,1024]{2,1,0:T(8,128)(2,1)} %param.20) | copy-start | bytes 786436
  415.8 6.1 %copy-start.4 = (bf16[1,128,256]{2,1,0:T(8,128)(2,1)S(1)}, bf16[1,128,256]{2,1,0:T(8,128)(2,1)}, u32[]{:S(2)}) copy-start(bf16[1,128,256]{2,1,0:T(8,128)(2,1)} %param.21) | copy-start | bytes 196612
  415.8 6.4 %copy-start.2 = (bf16[1,128,2688]{2,1,0:T(8,128)(2,1)S(1)}, bf16[1,128,2688]{2,1,0:T(8,128)(2,1)}, u32[]{:S(2)}) copy-start(bf16[1,128,2688]{2,1,0:T(8,128)(2,1)} %param.23) | copy-start | bytes 2064388
  415.8 61.0 %all-to-all-start.1 = ((bf16[8,2,54,1344]{3,1,2,0:T(2,128)(2,1)}), bf16[8,2,54,1344]{3,1,2,0:T(2,128)(2,1)}, u32[]{:S(2)}, u32[]{:S(2)}) async-start(bf16[8,2,54,1344]{3,1,2,0:T(2,128)(2,1)} %copy.96), calls=%async_computation.1 | async-start | bytes 4866048 | tf_op jit(solution)/shard_map/all_to_all | solution.py:174
  421.4 32.1 %reduce-scatter.2.cloned.1.call-start = ((), (), s32[]{:S(2)}) async-start(), calls=%async_computation.5 | async-start | bytes 1032192 | tf_op jit(solution)/shard_map/reduce_scatter | solution.py:164
  421.8 4.8 copy-start.15
  434.2 2.6 copy-start.6
  453.5 34.3 %collective-permute-start.1 = (bf16[128,1344]{0,1:T(8,128)(2,1)}, bf16[128,1344]{0,1:T(8,128)(2,1)S(1)}, u32[]{:S(2)}, u32[]{:S(2)}) collective-permute-start(bf16[128,1344]{0,1:T(8,128)(2,1)} %reduce-scatter.2.cloned.1.call-done), channel_id=1, source_target_pairs={{0,16},{16,0},{1,17},{17,1},{2,18},{18,2},{3,19},{19,3},{4,20},{20... | collective-permute-start | bytes 1032200 | tf_op jit(solution)/shard_map/ppermute | solution.py:21
  480.3 4.4 copy-start.8
  480.3 4.4 copy-start.10
  480.3 4.4 copy-start.12
  480.3 4.4 copy-start.14
  487.7 1.7 collective-permute-start
Sparse Core Ops, SparseCore 0:
  127.9 134.2 all-gather.2
  294.8 95.1 all-gather.4
  436.9 16.5 reduce-scatter.1
where the time goes:
time: 499 us; the launch traced here: 497 us
  waiting for transfers between devices  322 us (65%)
  local copies, waits for them, and re-layouts  74 us (15%)
  matrix products  62.6 us (13%)
  between operations  14.1 us (3%)
  starting transfers between devices  13.5 us (3%)
  other arithmetic  6.66 us (1%)
    all_gather x1, waiting for transfers between devices, on_device(): piece = lax.all_gather(scaled, 'dp', axis=3, tiled=True)  129 us
    all_gather x1, waiting for transfers between devices, on_device(): lax.all_gather(hidden, 'dp', axis=3, tiled=True)  95.3 us
    all_to_all x1, waiting for transfers between devices, on_device(): lax.all_to_all(outgoing, 'expert', split_axis=0, concat_axis=0, tiled=True)  55.4 us
    reshape x2, local copies, waits for them, and re-layouts, on_device(): outgoing = outgoing.reshape(columns, local_experts, capacity, feature_share)  37 us
    all_to_all x1, waiting for transfers between devices, on_device(): lax.all_to_all(expert_rows, 'expert', split_axis=0, concat_axis=0, tiled=...  23.2 us
    dot_general x2, matrix products, block_product(): jnp.einsum('sjcw,jwh->sjch', block_rows, weight_rows, preferred_element_t...  21.2 us
    dot_general x1, matrix products, on_device(): jnp.einsum('sjch,jhd->sjcd', lax.all_gather(hidden, 'dp', axis=3, tiled=T...  20.2 us
    reduce_scatter x1, waiting for transfers between devices, on_device(): lax.psum_scatter(grad_term.astype(jnp.bfloat16), 'dp', scatter_dimension=...  16.7 us
  transfers between devices with their start and end apart: 7, of which 6 were waited for; matrix products, arithmetic and copies ran while one was open for 5% of the time, Pallas kernels for 0%

commit v1 on v0

--- a/solution.py
+++ b/solution.py
@@ -148,7 +148,14 @@
     gain_part = lax.dynamic_slice_in_dim(norm_gain, feature_index * feature_share, feature_share, 0)
     scaled = (arrived_wide * gain_part).astype(jnp.bfloat16)
     running = start_up
-    piece = lax.all_gather(scaled, "dp", axis=3, tiled=True)
+    ways, here = (lax.axis_size("dp"), lax.axis_index("dp"))
+    piece, reach = (scaled, 1)
+    while reach < ways:
+        theirs = lax.ppermute(piece, "dp", [(d, d ^ reach) for d in range(ways)])
+        mine_first = jnp.concatenate([piece, theirs], axis=3)
+        theirs_first = jnp.concatenate([theirs, piece], axis=3)
+        piece = jnp.where(here & reach == 0, mine_first, theirs_first)
+        reach = 2 * reach
     start = jnp.int32(0)
     for block_number in range(piece.shape[3] // feature_share):
         first = block_number * feature_share

time: 499 us -> 401 us (0.80)
  waiting for transfers between devices: 322 us -> 193 us
  blocking collectives: 4.96 us -> 52.4 us
  matrix products: 62.6 us -> 50.9 us
  local copies, waits for them, and re-layouts: 74 us -> 65.1 us
    all_gather x1 -> x0, waiting for transfers between devices: 129 us -> none  [on_device(): piece = lax.all_gather(scaled, 'dp', axis=3, tiled=True)]
    psum x1, blocking collectives: 4.96 us -> 52.4 us  [on_device(): squares = lax.psum(jnp.sum(jnp.square(arrived_wide), axis=3), 'dp')]
    dot_general x2, matrix products: 21.2 us -> 9.48 us  [block_product(): jnp.einsum('sjcw,jwh->sjch', block_rows, weight_rows, preferred_element_t...]
    convert_element_type x1, local copies, waits for them, and re-layouts: 8.93 us -> 1.72 us  [on_device(): scaled = (arrived_wide * gain_part).astype(jnp.bfloat16)]
    slice x2 -> x1, local copies, waits for them, and re-layouts: 5.75 us -> 0.25 us  [the longest x1 5.5 us: on_device(): piece[:, :, :, first:first + feature_share]]
  transfers between devices with their start and end apart: 7 -> 7, of which waited for: 6 -> 5; matrix products, arithmetic and copies ran while one was open for 5% -> 6% of each run, Pallas kernels for 0% -> 0%
where the time goes in v1:
time: 401 us; the launch traced here: 400 us
  waiting for transfers between devices  193 us (48%)
  local copies, waits for them, and re-layouts  65.1 us (16%)
  blocking collectives  52.4 us (13%)
  matrix products  50.9 us (13%)
  starting transfers between devices  15 us (4%)
  between operations  14.4 us (4%)
  other arithmetic  10 us (2%)
    all_gather x1, waiting for transfers between devices, on_device(): lax.all_gather(hidden, 'dp', axis=3, tiled=True)  95.6 us
    all_to_all x1, waiting for transfers between devices, on_device(): lax.all_to_all(outgoing, 'expert', split_axis=0, concat_axis=0, tiled=True)  55.4 us
    psum x1, blocking collectives, on_device(): squares = lax.psum(jnp.sum(jnp.square(arrived_wide), axis=3), 'dp')  52.4 us
    reshape x2, local copies, waits for them, and re-layouts, on_device(): outgoing = outgoing.reshape(columns, local_experts, capacity, feature_share)  37 us
    all_to_all x1, waiting for transfers between devices, on_device(): lax.all_to_all(expert_rows, 'expert', split_axis=0, concat_axis=0, tiled=...  23.2 us
    dot_general x1, matrix products, on_device(): jnp.einsum('sjch,jhd->sjcd', lax.all_gather(hidden, 'dp', axis=3, tiled=T...  20.2 us
    reduce_scatter x1, waiting for transfers between devices, on_device(): lax.psum_scatter(grad_term.astype(jnp.bfloat16), 'dp', scatter_dimension=...  16.7 us
    dot_general x2, matrix products, block_product(): jnp.einsum('sjcw,jwh->sjch', block_rows, weight_rows, preferred_element_t...  9.48 us
  transfers between devices with their start and end apart: 7, of which 5 were waited for; matrix products, arithmetic and copies ran while one was open for 6% of the time, Pallas kernels for 0%

profile of v1, /device:TPU:0, one launch (start us, length us, event | category | flops | bytes accessed | tf_op | source)
XLA Modules:
  0.0 400.4 jit_solution(7664096428616999825)
XLA Ops:
  7.2 0.9 copy.43
  8.4 1.7 reduce-window.6
  11.5 3.5 convolution_convert_fusion
  15.0 21.9 %reshape.76 = bf16[8,2,54,1344]{2,1,0,3:T(2,128)(2,1)} reshape(bf16[864,1344]{0,1:T(8,128)(2,1)} %convolution_convert_fusion) | data formatting | bytes 4644864 | tf_op jit(solution)/shard_map/reshape | solution.py:143
  36.9 15.1 %copy.48 = bf16[8,2,54,1344]{3,1,2,0:T(2,128)(2,1)} copy(bf16[8,2,54,1344]{2,1,0,3:T(2,128)(2,1)} %reshape.76) | data formatting | bytes 4644864 | tf_op jit(solution)/shard_map/reshape | solution.py:143
  52.0 7.4 %all-to-all-start = ((bf16[8,2,54,1344]{3,1,2,0:T(2,128)(2,1)}), bf16[8,2,54,1344]{3,1,2,0:T(2,128)(2,1)}, u32[]{:S(2)}, u32[]{:S(2)}) async-start(bf16[8,2,54,1344]{3,1,2,0:T(2,128)(2,1)} %copy.48), calls=%async_computation | async-start | bytes 4866048 | tf_op jit(solution)/shard_map/all_to_all | solution.py:144
  59.5 55.4 %all-to-all-done = bf16[8,2,54,1344]{3,1,2,0:T(2,128)(2,1)} async-done(((bf16[8,2,54,1344]{3,1,2,0:T(2,128)(2,1)}), bf16[8,2,54,1344]{3,1,2,0:T(2,128)(2,1)}, u32[]{:S(2)}, u32[]{:S(2)}) %all-to-all-start) | async-done | bytes 2322464 | tf_op jit(solution)/shard_map/all_to_all | solution.py:144
  115.0 2.6 fusion.11
  117.5 1.5 copy-done.1
  119.0 1.7 copy.50
  120.7 1.5 collective-permute-start
  122.2 52.4 %psum.7 = f32[8,2,54]{2,0,1:T(8,128)S(1)} all-reduce(f32[8,2,54]{2,0,1:T(8,128)S(1)} %get-tuple-element.8), channel_id=1, replica_groups=mesh['segment'=2,'expert'=8,'dp'=2] {'dp'}, use_global_device_ids=true, to_apply=%region_5.6 | all-reduce | flops 864 | bytes 6912 | tf_op jit(solution)/shard_map/psum | solution.py:147
  174.6 2.1 copy.51
  177.0 4.7 %maximum_select_fusion = bf16[8,2,54,2688]{3,2,0,1:T(8,128)(2,1)S(1)} fusion(bf16[8,2,54,1344]{3,2,0,1:T(8,128)(2,1)S(1)} %copy.51, bf16[8,2,54,1344]{3,2,0,1:T(8,128)(2,1)S(1)} %copy-done.2, pred[]{:T(512)S(6)} %eq.150), kind=kLoop, calls=%fused_computation.14 | loop fusion | flops 20901888 | bytes 9289729 | tf_op jit(solution)/shard_map/jit(_where)/select_n | solution.py:157
  181.8 5.6 %convert_bitcast_fusion.1 = bf16[8,2,54,928]{3,2,0,1:T(8,128)(2,1)S(1)} fusion(bf16[2,2688,928]{1,2,0:T(8,128)(2,1)} %param.18, bf16[8,2,54,2688]{3,2,0,1:T(8,128)(2,1)S(1)} %maximum_select_fusion), kind=kOutput, calls=%fused_computation.26 | convolution fusion | flops 2156018688 | bytes 9353216 | tf_op jit(solution)/shard_map/sjcw,jwh->sjch/dot_general | solution.py:84
  187.4 3.8 convert_bitcast_fusion
  192.1 4.9 %copy.53 = bf16[8,2,54,928]{2,0,1,3:T(8,128)(2,1)} copy(bf16[8,2,54,928]{3,2,0,1:T(8,128)(2,1)S(1)} %multiply_convert_fusion) | data formatting | bytes 3207168 | tf_op jit(solution)/shard_map/convert_element_type | solution.py:167
  197.0 95.6 %all-gather.2.cloned.1.call-done = bf16[8,2,54,1856]{2,0,1,3:T(8,128)(2,1)} async-done(((bf16[8,2,54,928]{2,0,1,3:T(8,128)(2,1)}), bf16[8,2,54,1856]{2,0,1,3:T(8,128)(2,1)}) %all-gather.2.cloned.1.call-update) | async-done | bytes 3207184 | tf_op jit(solution)/shard_map/all_gather | solution.py:176
  292.6 20.2 %fusion.18 = bf16[8,2,54,1344]{3,2,0,1:T(8,128)(2,1)} fusion(bf16[2,1856,1344]{1,2,0:T(8,128)(2,1)} %param.19, bf16[8,2,54,1856]{2,0,1,3:T(8,128)(2,1)} %all-gather.2.cloned.1.call-done), kind=kOutput, calls=%fused_computation.21 | convolution fusion | flops 4311595008 | bytes 15507456 | tf_op jit(solution)/shard_map/sjch,jhd->sjcd/dot_general | solution.py:174
  312.8 5.7 %copy.55 = bf16[8,2,54,1344]{3,1,2,0:T(2,128)(2,1)} copy(bf16[8,2,54,1344]{3,2,0,1:T(8,128)(2,1)} %fusion.18) | data formatting | bytes 4644864 | tf_op jit(solution)/shard_map/convert_element_type | solution.py:180
  318.4 5.6 %all-to-all-start.1 = ((bf16[8,2,54,1344]{3,1,2,0:T(2,128)(2,1)}), bf16[8,2,54,1344]{3,1,2,0:T(2,128)(2,1)}, u32[]{:S(2)}, u32[]{:S(2)}) async-start(bf16[8,2,54,1344]{3,1,2,0:T(2,128)(2,1)} %copy.55), calls=%async_computation.1 | async-start | bytes 4866048 | tf_op jit(solution)/shard_map/all_to_all | solution.py:181
  324.9 4.4 %fusion.38 = bf16[16,8,8,128]{3,2,1,0:T(8,128)(2,1)S(1)} fusion(bf16[1024,2688]{1,0:T(8,128)(2,1)} %param.27, bf16[1,128,2688]{2,1,0:T(8,128)(2,1)S(1)} %copy-done.3), kind=kOutput, calls=%fused_computation.36 | convolution fusion | flops 704774144 | bytes 6455296 | tf_op jit(solution)/shard_map/td,qd->tq/dot_general | solution.py:36
  329.7 1.0 fusion.37
  330.6 1.6 fusion.42
  332.3 4.6 %convolution_add_fusion = f32[128,2688]{0,1:T(8,128)S(1)} fusion(f32[128,2688]{0,1:T(8,128)} %fusion.42, bf16[2688,1024]{1,0:T(8,128)(2,1)} %param.24, bf16[128,1024]{0,1:T(8,128)(2,1)} %bitcast.152), kind=kOutput, calls=%fused_computation.15 | convolution fusion | flops 704987136 | bytes 8519680 | tf_op jit(solution)/shard_map/tq,dq->td/dot_general | solution.py:71
  336.9 2.5 fusion.12
  339.6 16.7 %reduce-scatter.2.cloned.1.call-done = bf16[128,1344]{0,1:T(8,128)(2,1)} async-done(((bf16[128,2688]{0,1:T(8,128)(2,1)}), bf16[128,1344]{0,1:T(8,128)(2,1)}) %reduce-scatter.2.cloned.1.call-update) | async-done | bytes 344080 | tf_op jit(solution)/shard_map/reduce_scatter | solution.py:171
  356.2 23.2 %all-to-all-done.1 = bf16[8,2,54,1344]{3,1,2,0:T(2,128)(2,1)} async-done(((bf16[8,2,54,1344]{3,1,2,0:T(2,128)(2,1)}), bf16[8,2,54,1344]{3,1,2,0:T(2,128)(2,1)}, u32[]{:S(2)}, u32[]{:S(2)}) %all-to-all-start.1) | async-done | bytes 2322464 | tf_op jit(solution)/shard_map/all_to_all | solution.py:181
  379.5 3.5 copy.56
  382.9 4.4 %reshape.65 = bf16[864,1344]{1,0:T(8,128)(2,1)} reshape(bf16[8,2,54,1344]{3,2,1,0:T(8,128)(2,1)} %copy.56) | data formatting | bytes 4644864 | tf_op jit(solution)/shard_map/reshape | solution.py:183
  387.4 3.0 convolution_convert_fusion.1
  390.5 1.6 collective-permute-done.1
  (71 shorter events, 5.5 us)
Async XLA Ops:
  7.2 323.5 %copy-start = (bf16[2688,256]{1,0:T(8,128)(2,1)S(1)}, bf16[2688,256]{1,0:T(8,128)(2,1)}, u32[]{:S(2)}) copy-start(bf16[2688,256]{1,0:T(8,128)(2,1)} %param.25) | copy-start | bytes 4128772
  10.9 0.5 copy-start.8
  10.9 0.6 copy-start.10
  10.9 0.6 copy-start.12
  11.0 0.6 copy-start.14
  52.0 7.5 %copy-start.6 = (f32[2688]{0:T(1024)S(1)}, f32[2688]{0:T(1024)}, u32[]{:S(2)}) copy-start(f32[2688]{0:T(1024)} %param.15) | copy-start | bytes 32260
  52.0 63.0 %all-to-all-start = ((bf16[8,2,54,1344]{3,1,2,0:T(2,128)(2,1)}), bf16[8,2,54,1344]{3,1,2,0:T(2,128)(2,1)}, u32[]{:S(2)}, u32[]{:S(2)}) async-start(bf16[8,2,54,1344]{3,1,2,0:T(2,128)(2,1)} %copy.48), calls=%async_computation | async-start | bytes 4866048 | tf_op jit(solution)/shard_map/all_to_all | solution.py:144
  59.4 233.2 %all-gather.2.cloned.1.call-start = ((), (), s32[]{:S(2)}) async-start(), calls=%async_computation.3 | async-start | bytes 11403264 | tf_op jit(solution)/shard_map/all_gather | solution.py:176
  117.5 1.5 copy-start.1
  120.7 53.9 %collective-permute-start = (bf16[8,2,54,1344]{3,0,2,1:T(8,128)(2,1)}, bf16[8,2,54,1344]{3,0,2,1:T(8,128)(2,1)}, u32[]{:S(2)}, u32[]{:S(2)}) collective-permute-start(bf16[8,2,54,1344]{3,0,2,1:T(8,128)(2,1)} %copy.50), channel_id=1, source_target_pairs={{0,1},{1,0},{2,3},{3,2},{4,5},{5,4},{6,7},{7,6},{8,9},{9,8},{10,11... | collective-permute-start | bytes 6967304 | tf_op jit(solution)/shard_map/ppermute | solution.py:154
  174.6 2.4 copy-start.2
  177.0 10.4 %slice-start = ((s8[9977856]{0:T(1024)(128)(4,1)}), s8[4194304]{0:T(1024)(128)(4,1)S(1)}, s32[]{:S(2)}) async-start(s8[9977856]{0:T(1024)(128)(4,1)} %bitcast.159), calls=%async_computation.5 | async-start | bytes 8388608
  177.0 10.4 %slice-start.1 = ((s8[9977856]{0:T(1024)(128)(4,1)}), s8[4194304]{0:T(1024)(128)(4,1)S(1)}, s32[]{:S(2)}) async-start(s8[9977856]{0:T(1024)(128)(4,1)} %bitcast.159), calls=%async_computation.6 | async-start | bytes 8388608
  181.7 5.7 %slice-start.2 = ((s8[9977856]{0:T(1024)(128)(4,1)}), s8[1589248]{0:T(1024)(128)(4,1)S(1)}, s32[]{:S(2)}) async-start(s8[9977856]{0:T(1024)(128)(4,1)} %bitcast.159), calls=%async_computation.7 | async-start | bytes 3178496
  318.4 6.0 %copy-start.4 = (bf16[1,128,1024]{2,1,0:T(8,128)(2,1)S(1)}, bf16[1,128,1024]{2,1,0:T(8,128)(2,1)}, u32[]{:S(2)}) copy-start(bf16[1,128,1024]{2,1,0:T(8,128)(2,1)} %param.20) | copy-start | bytes 786436
  318.4 6.1 %copy-start.5 = (bf16[1,128,256]{2,1,0:T(8,128)(2,1)S(1)}, bf16[1,128,256]{2,1,0:T(8,128)(2,1)}, u32[]{:S(2)}) copy-start(bf16[1,128,256]{2,1,0:T(8,128)(2,1)} %param.21) | copy-start | bytes 196612
  318.4 6.4 %copy-start.3 = (bf16[1,128,2688]{2,1,0:T(8,128)(2,1)S(1)}, bf16[1,128,2688]{2,1,0:T(8,128)(2,1)}, u32[]{:S(2)}) copy-start(bf16[1,128,2688]{2,1,0:T(8,128)(2,1)} %param.23) | copy-start | bytes 2064388
  318.4 61.0 %all-to-all-start.1 = ((bf16[8,2,54,1344]{3,1,2,0:T(2,128)(2,1)}), bf16[8,2,54,1344]{3,1,2,0:T(2,128)(2,1)}, u32[]{:S(2)}, u32[]{:S(2)}) async-start(bf16[8,2,54,1344]{3,1,2,0:T(2,128)(2,1)} %copy.55), calls=%async_computation.1 | async-start | bytes 4866048 | tf_op jit(solution)/shard_map/all_to_all | solution.py:181
  324.1 32.1 %reduce-scatter.2.cloned.1.call-start = ((), (), s32[]{:S(2)}) async-start(), calls=%async_computation.4 | async-start | bytes 1032192 | tf_op jit(solution)/shard_map/reduce_scatter | solution.py:171
  324.5 4.8 %copy-start.16 = (bf16[1,128,256]{2,1,0:T(8,128)(2,1)S(1)}, bf16[1,128,256]{2,1,0:T(8,128)(2,1)}, u32[]{:S(2)}) copy-start(bf16[1,128,256]{2,1,0:T(8,128)(2,1)} %param.22) | copy-start | bytes 196612
  336.9 2.6 copy-start.7
  356.2 34.2 %collective-permute-start.2 = (bf16[128,1344]{0,1:T(8,128)(2,1)}, bf16[128,1344]{0,1:T(8,128)(2,1)S(1)}, u32[]{:S(2)}, u32[]{:S(2)}) collective-permute-start(bf16[128,1344]{0,1:T(8,128)(2,1)} %reduce-scatter.2.cloned.1.call-done), channel_id=1, source_target_pairs={{0,16},{16,0},{1,17},{17,1},{2,18},{18,2},{3,19},{19,3},{4,20},{20... | collective-permute-start | bytes 1032200 | tf_op jit(solution)/shard_map/ppermute | solution.py:21
  382.9 4.4 %copy-start.9 = (s32[128]{0:T(128)S(1)}, s32[128]{0:T(128)}, u32[]{:S(2)}) copy-start(s32[128]{0:T(128)} %copy-done.8) | copy-start | bytes 1540
  382.9 4.4 %copy-start.11 = (s32[128]{0:T(128)S(1)}, s32[128]{0:T(128)}, u32[]{:S(2)}) copy-start(s32[128]{0:T(128)} %copy-done.10) | copy-start | bytes 1540
  382.9 4.4 %copy-start.13 = (s32[128]{0:T(128)S(1)}, s32[128]{0:T(128)}, u32[]{:S(2)}) copy-start(s32[128]{0:T(128)} %copy-done.12) | copy-start | bytes 1540
  382.9 4.4 %copy-start.15 = (s32[128]{0:T(128)S(1)}, s32[128]{0:T(128)}, u32[]{:S(2)}) copy-start(s32[128]{0:T(128)} %copy-done.14) | copy-start | bytes 1540
  390.4 1.7 collective-permute-start.1
Sparse Core Ops, SparseCore 0:
  197.1 95.4 all-gather.1
  339.6 16.5 reduce-scatter.1
